TPU v7x, 256 devices: a whole 4x4x8 slice. The times are simulated.
256 devices in a mesh: dp: 16 (over z, x_lo), ctx: 16 (over x_hi, y, core).
Axes of the slice: x: 4 (x_hi: 2, x_lo: 2; x = x_hi * 2 + x_lo), y: 4, z: 8, core: 2. Of those that a mesh axis runs over, the one named last changes fastest.
Arguments:
- normed: bfloat16 [16, 4096, 2048], P('dp', 'ctx'), may hold values from -21 to 21
- token_ids: int32 [16, 4096], P('dp', 'ctx'), may hold values from 0 to 128255
- block_order: int32 [16], replicated, may hold values from 0 to 15, each once
- master_weight: float32 [2048, 3072], P(('dp', 'ctx')), may hold values from -0.125 to 0.125
- weight_grad: float32 [2048, 3072], P(('dp', 'ctx')), may hold values from -6 to 6
- moment_one: float32 [2048, 3072], P(('dp', 'ctx')), may hold values from -4 to 4
- moment_two: float32 [2048, 3072], P(('dp', 'ctx')), may hold values from 0.1 to 3
Outputs:
- new_master: float32 [2048, 3072], P(('dp', 'ctx'))
- new_moment_one: float32 [2048, 3072], P(('dp', 'ctx'))
- new_moment_two: float32 [2048, 3072], P(('dp', 'ctx'))
- attended: bfloat16 [16, 4096, 2048], P('dp', 'ctx')
All inputs are finite; a program needn't handle non-finite values.
Results may differ from a plain program's by a relative error of at most 0.008.
The roundings to bfloat16 on the way count: a program that leaves them out, or rounds other values in their place, can miss the bound.
Values may be sent and summed in bfloat16 or wider, within the bound.
A program may use at most 64 MiB of HBM per device.

v0:
```python
import jax
import jax.numpy as jnp
from jax import lax
from jax.sharding import PartitionSpec as P

HQ = 16
HK = 4
DH = 128
GROUP = 4
beta_one = 0.9
beta_two = 0.95
adam_step = 10.0
learn_rate = 0.0003
decay_rate = 0.1
adam_eps = 1e-08
rope_theta = 500000.0
masked_score = -1e30


def passed_along(x, axis, by):
    count = lax.axis_size(axis)
    return lax.ppermute(x, axis, [(i, (i + by) % count) for i in range(count)])


def adam_update(master_weight, weight_grad, moment_one, moment_two):
    fresh_one = beta_one * moment_one + (1.0 - beta_one) * weight_grad
    fresh_two = beta_two * moment_two + (1.0 - beta_two) * weight_grad * weight_grad
    fix_one = 1.0 - beta_one**adam_step
    fix_two = 1.0 - beta_two**adam_step
    step_size = fresh_one / fix_one / (jnp.sqrt(fresh_two / fix_two) + adam_eps)
    fresh_master = master_weight - learn_rate * (step_size + decay_rate * master_weight)
    return (fresh_master, fresh_one, fresh_two)


def rotate(values, positions):
    half_dim = values.shape[-1] // 2
    frequency = rope_theta ** (-2.0 * jnp.arange(half_dim, dtype=jnp.float32) / values.shape[-1])
    angles = positions.astype(jnp.float32)[:, None] * frequency[None, :]
    cosine = jnp.cos(angles)[:, None, :]
    sine_part = jnp.sin(angles)[:, None, :]
    first_half = values[..., :half_dim]
    second_half = values[..., half_dim:]
    return jnp.concatenate(
        [
            first_half * cosine - second_half * sine_part,
            second_half * cosine + first_half * sine_part,
        ],
        -1,
    )


def local(normed, token_ids, block_order, master_weight, weight_grad, moment_one, moment_two):
    new_master, new_moment_one, new_moment_two = adam_update(
        master_weight, weight_grad, moment_one, moment_two
    )
    fresh_weight = new_master.astype(jnp.bfloat16)
    tok_rows = normed[0]
    block_len = tok_rows.shape[0]
    projected = jnp.dot(
        tok_rows,
        lax.all_gather(fresh_weight, ("dp", "ctx"), axis=0, tiled=True),
        preferred_element_type=jnp.float32,
    )
    place = lax.axis_index("ctx")
    place_count = lax.axis_size("ctx")
    local_idx = jnp.arange(block_len, dtype=jnp.int32)
    my_block = block_order[place]
    positions = my_block * block_len + local_idx
    doc_gap = block_len * place_count // 2
    marks = jnp.where(token_ids[0] % doc_gap == 0, positions, 0)
    last_mark = jnp.max(marks)
    all_marks = lax.all_gather(last_mark[None], "ctx", axis=0, tiled=True)
    prior_mark = jnp.max(jnp.where(block_order < my_block, all_marks, 0))
    doc_start = jnp.maximum(lax.cummax(marks, axis=0), prior_mark)
    queries = rotate(projected[:, : HQ * DH].reshape(block_len, HQ, DH), positions).astype(
        jnp.bfloat16
    )
    key_rows = rotate(
        projected[:, HQ * DH : (HQ + HK) * DH].reshape(block_len, HK, DH), positions
    ).astype(jnp.bfloat16)
    value_rows = projected[:, (HQ + HK) * DH :].astype(jnp.bfloat16)
    key_block = jnp.concatenate([key_rows.reshape(block_len, HK * DH), value_rows], 1)
    score_scale = DH ** (-0.5)

    def attend_head(carry, kv_head, key_part, value_part, key_pos):
        run_max, run_sum, run_acc = carry
        group_q = queries[:, kv_head * GROUP : (kv_head + 1) * GROUP, :]
        scores = (
            jnp.einsum("qjd,kd->jqk", group_q, key_part, preferred_element_type=jnp.float32)
            * score_scale
        )
        allowed = (key_pos[None, :] <= positions[:, None]) & (
            key_pos[None, :] >= doc_start[:, None]
        )
        scores = jnp.where(allowed[None], scores, masked_score)
        new_max = jnp.maximum(run_max, jnp.max(scores, -1))
        weights = jnp.where(allowed[None], jnp.exp(scores - new_max[..., None]), 0.0)
        factor = jnp.exp(run_max - new_max)
        run_sum = run_sum * factor + jnp.sum(weights, -1)
        run_acc = run_acc * factor[..., None] + jnp.einsum(
            "jqk,kd->jqd",
            weights.astype(jnp.bfloat16),
            value_part,
            preferred_element_type=jnp.float32,
        )
        return (new_max, run_sum, run_acc)

    def attend_block(carries, moving, source, head_list):
        key_pos = block_order[source] * block_len + local_idx
        head_count = len(head_list)
        updated = list(carries)
        for slot, kv_head in enumerate(head_list):
            key_part = moving[:, slot * DH : (slot + 1) * DH]
            value_part = moving[:, (head_count + slot) * DH : (head_count + slot + 1) * DH]
            updated[kv_head] = attend_head(carries[kv_head], kv_head, key_part, value_part, key_pos)
        return tuple(updated)

    start_state = (
        jnp.full((GROUP, block_len), masked_score, jnp.float32),
        jnp.zeros((GROUP, block_len), jnp.float32),
        jnp.zeros((GROUP, block_len, DH), jnp.float32),
    )
    carries = tuple((start_state for kv_head in range(HK)))
    every_head = list(range(HK))
    carries = attend_block(carries, key_block, place, every_head)

    def one_step(step_idx, state):
        held, moving = state
        moving = passed_along(moving, "ctx", 1)
        source = (place - step_idx - 1) % place_count
        return (attend_block(held, moving, source, every_head), moving)

    carries, unused_block = lax.fori_loop(0, place_count - 1, one_step, (carries, key_block))
    head_outputs = []
    for kv_head in range(HK):
        run_max, run_sum, run_acc = carries[kv_head]
        normalized = run_acc / run_sum[..., None]
        head_outputs.append(jnp.transpose(normalized, (1, 0, 2)).reshape(block_len, GROUP * DH))
    attended = jnp.concatenate(head_outputs, 1).astype(jnp.bfloat16)
    return (new_master, new_moment_one, new_moment_two, attended[None])


def solution(mesh):
    in_specs = (
        P("dp", "ctx", None),
        P("dp", "ctx"),
        P(),
        P(("dp", "ctx"), None),
        P(("dp", "ctx"), None),
        P(("dp", "ctx"), None),
        P(("dp", "ctx"), None),
    )
    out_specs = (
        P(("dp", "ctx"), None),
        P(("dp", "ctx"), None),
        P(("dp", "ctx"), None),
        P("dp", "ctx", None),
    )
    return jax.shard_map(local, mesh=mesh, in_specs=in_specs, out_specs=out_specs, check_vma=False)
```

profile of v0, /device:TPU:32, one launch (start us, length us, event | category | flops | bytes accessed | tf_op | source)
XLA Modules:
  0.0 757.4 jit_solution(6095916171341330654)
XLA Ops:
  17.4 14.1 %all-reduce = s32[16]{0:T(128)S(1)} all-reduce(s32[16]{0:T(128)S(1)} %dynamic-update-slice), channel_id=1, replica_groups=mesh['dp'=16,'ctx'=16] {'ctx'}, use_global_device_ids=true, to_apply=%add | all-reduce | flops 16 | bytes 128
  34.5 402.0 %all-gather.2.cloned.1.call-done = bf16[2048,3072]{1,0:T(8,128)(2,1)} async-done(((bf16[8,3072]{1,0:T(8,128)(2,1)}), bf16[2048,3072]{1,0:T(8,128)(2,1)}) %all-gather.2.cloned.1.call-update) | async-done | bytes 12582928 | tf_op jit(solution)/shard_map/all_gather | solution.py:61
  436.5 9.7 %fusion.118 = (bf16[256,3072]{0,1:T(8,128)(2,1)}, f32[256,3072]{0,1:T(8,128)S(1)}) fusion(bf16[2048,3072]{1,0:T(8,128)(2,1)} %all-gather.2.cloned.1.call-done, bf16[1,256,2048]{2,1,0:T(8,128)(2,1)S(1)} %copy-done), kind=kOutput, calls=%fused_computation.202 | convolution fusion | flops 3222011904 | bytes 18350080 | tf_op jit(solution)/shard_map/dot_general | solution.py:59
  450.5 3.2 copy.111
  454.8 2.2 add_convert_fusion
  462.4 2.1 convolution_add_fusion.6
  464.5 2.1 convolution_add_fusion.5
  466.6 2.1 convolution_add_fusion.4
  469.8 276.4 %while.40 = (s32[]{:T(128)}, f32[4,256]{1,0:T(4,128)S(1)}, f32[4,256]{1,0:T(4,128)S(1)}, f32[4,256,128]{2,1,0:T(8,128)S(1)}, f32[4,256]{1,0:T(4,128)S(1)}, /*ind...) while((s32[]{:T(128)}, f32[4,256]{1,0:T(4,128)S(1)}, ...), condition=%wide.region_21.22_spmd.clone, body=%wide.region_12.21_spmd.clone.sunk | while | flops 547561984 | bytes 35001972 | solution.py:133
  471.1 11.1 %collective-permute-done = bf16[256,1024]{1,0:T(8,128)(2,1)S(1)} collective-permute-done((bf16[256,1024]{1,0:T(8,128)(2,1)}, bf16[256,1024]{1,0:T(8,128)(2,1)S(1)}, u32[]{:S(2)}, u32[]{:S(2)}) %collective-permute-start) | collective-permute-done | bytes 524320 | tf_op jit(solution)/shard_map/while/body/eval_jaxpr/ppermute | solution.py:22
  489.6 11.1 %collective-permute-done = bf16[256,1024]{1,0:T(8,128)(2,1)S(1)} collective-permute-done((bf16[256,1024]{1,0:T(8,128)(2,1)}, bf16[256,1024]{1,0:T(8,128)(2,1)S(1)}, u32[]{:S(2)}, u32[]{:S(2)}) %collective-permute-start) | collective-permute-done | bytes 524320 | tf_op jit(solution)/shard_map/while/body/eval_jaxpr/ppermute | solution.py:22
  508.0 11.1 %collective-permute-done = bf16[256,1024]{1,0:T(8,128)(2,1)S(1)} collective-permute-done((bf16[256,1024]{1,0:T(8,128)(2,1)}, bf16[256,1024]{1,0:T(8,128)(2,1)S(1)}, u32[]{:S(2)}, u32[]{:S(2)}) %collective-permute-start) | collective-permute-done | bytes 524320 | tf_op jit(solution)/shard_map/while/body/eval_jaxpr/ppermute | solution.py:22
  526.4 11.1 %collective-permute-done = bf16[256,1024]{1,0:T(8,128)(2,1)S(1)} collective-permute-done((bf16[256,1024]{1,0:T(8,128)(2,1)}, bf16[256,1024]{1,0:T(8,128)(2,1)S(1)}, u32[]{:S(2)}, u32[]{:S(2)}) %collective-permute-start) | collective-permute-done | bytes 524320 | tf_op jit(solution)/shard_map/while/body/eval_jaxpr/ppermute | solution.py:22
  544.8 11.1 %collective-permute-done = bf16[256,1024]{1,0:T(8,128)(2,1)S(1)} collective-permute-done((bf16[256,1024]{1,0:T(8,128)(2,1)}, bf16[256,1024]{1,0:T(8,128)(2,1)S(1)}, u32[]{:S(2)}, u32[]{:S(2)}) %collective-permute-start) | collective-permute-done | bytes 524320 | tf_op jit(solution)/shard_map/while/body/eval_jaxpr/ppermute | solution.py:22
  563.3 11.1 %collective-permute-done = bf16[256,1024]{1,0:T(8,128)(2,1)S(1)} collective-permute-done((bf16[256,1024]{1,0:T(8,128)(2,1)}, bf16[256,1024]{1,0:T(8,128)(2,1)S(1)}, u32[]{:S(2)}, u32[]{:S(2)}) %collective-permute-start) | collective-permute-done | bytes 524320 | tf_op jit(solution)/shard_map/while/body/eval_jaxpr/ppermute | solution.py:22
  581.7 11.1 %collective-permute-done = bf16[256,1024]{1,0:T(8,128)(2,1)S(1)} collective-permute-done((bf16[256,1024]{1,0:T(8,128)(2,1)}, bf16[256,1024]{1,0:T(8,128)(2,1)S(1)}, u32[]{:S(2)}, u32[]{:S(2)}) %collective-permute-start) | collective-permute-done | bytes 524320 | tf_op jit(solution)/shard_map/while/body/eval_jaxpr/ppermute | solution.py:22
  600.1 11.1 %collective-permute-done = bf16[256,1024]{1,0:T(8,128)(2,1)S(1)} collective-permute-done((bf16[256,1024]{1,0:T(8,128)(2,1)}, bf16[256,1024]{1,0:T(8,128)(2,1)S(1)}, u32[]{:S(2)}, u32[]{:S(2)}) %collective-permute-start) | collective-permute-done | bytes 524320 | tf_op jit(solution)/shard_map/while/body/eval_jaxpr/ppermute | solution.py:22
  618.5 11.1 %collective-permute-done = bf16[256,1024]{1,0:T(8,128)(2,1)S(1)} collective-permute-done((bf16[256,1024]{1,0:T(8,128)(2,1)}, bf16[256,1024]{1,0:T(8,128)(2,1)S(1)}, u32[]{:S(2)}, u32[]{:S(2)}) %collective-permute-start) | collective-permute-done | bytes 524320 | tf_op jit(solution)/shard_map/while/body/eval_jaxpr/ppermute | solution.py:22
  637.0 11.1 %collective-permute-done = bf16[256,1024]{1,0:T(8,128)(2,1)S(1)} collective-permute-done((bf16[256,1024]{1,0:T(8,128)(2,1)}, bf16[256,1024]{1,0:T(8,128)(2,1)S(1)}, u32[]{:S(2)}, u32[]{:S(2)}) %collective-permute-start) | collective-permute-done | bytes 524320 | tf_op jit(solution)/shard_map/while/body/eval_jaxpr/ppermute | solution.py:22
  655.4 11.1 %collective-permute-done = bf16[256,1024]{1,0:T(8,128)(2,1)S(1)} collective-permute-done((bf16[256,1024]{1,0:T(8,128)(2,1)}, bf16[256,1024]{1,0:T(8,128)(2,1)S(1)}, u32[]{:S(2)}, u32[]{:S(2)}) %collective-permute-start) | collective-permute-done | bytes 524320 | tf_op jit(solution)/shard_map/while/body/eval_jaxpr/ppermute | solution.py:22
  673.8 11.1 %collective-permute-done = bf16[256,1024]{1,0:T(8,128)(2,1)S(1)} collective-permute-done((bf16[256,1024]{1,0:T(8,128)(2,1)}, bf16[256,1024]{1,0:T(8,128)(2,1)S(1)}, u32[]{:S(2)}, u32[]{:S(2)}) %collective-permute-start) | collective-permute-done | bytes 524320 | tf_op jit(solution)/shard_map/while/body/eval_jaxpr/ppermute | solution.py:22
  692.3 11.1 %collective-permute-done = bf16[256,1024]{1,0:T(8,128)(2,1)S(1)} collective-permute-done((bf16[256,1024]{1,0:T(8,128)(2,1)}, bf16[256,1024]{1,0:T(8,128)(2,1)S(1)}, u32[]{:S(2)}, u32[]{:S(2)}) %collective-permute-start) | collective-permute-done | bytes 524320 | tf_op jit(solution)/shard_map/while/body/eval_jaxpr/ppermute | solution.py:22
  710.7 11.1 %collective-permute-done = bf16[256,1024]{1,0:T(8,128)(2,1)S(1)} collective-permute-done((bf16[256,1024]{1,0:T(8,128)(2,1)}, bf16[256,1024]{1,0:T(8,128)(2,1)S(1)}, u32[]{:S(2)}, u32[]{:S(2)}) %collective-permute-start) | collective-permute-done | bytes 524320 | tf_op jit(solution)/shard_map/while/body/eval_jaxpr/ppermute | solution.py:22
  729.1 11.1 %collective-permute-done = bf16[256,1024]{1,0:T(8,128)(2,1)S(1)} collective-permute-done((bf16[256,1024]{1,0:T(8,128)(2,1)}, bf16[256,1024]{1,0:T(8,128)(2,1)S(1)}, u32[]{:S(2)}, u32[]{:S(2)}) %collective-permute-start) | collective-permute-done | bytes 524320 | tf_op jit(solution)/shard_map/while/body/eval_jaxpr/ppermute | solution.py:22
  (621 shorter events, 127.0 us)
Async XLA Ops:
  7.2 429.3 %copy-start = (bf16[1,256,2048]{2,1,0:T(8,128)(2,1)S(1)}, bf16[1,256,2048]{2,1,0:T(8,128)(2,1)}, u32[]{:S(2)}) copy-start(bf16[1,256,2048]{2,1,0:T(8,128)(2,1)} %param.9) | copy-start | bytes 3145732
  7.2 429.3 %all-gather.2.cloned.1.call-start = ((), (), s32[]{:S(2)}) async-start(), calls=%async_computation | async-start | bytes 12632064 | tf_op jit(solution)/shard_map/all_gather | solution.py:61
  466.6 3.2 copy-start.9
  469.8 12.4 %collective-permute-start = (bf16[256,1024]{1,0:T(8,128)(2,1)}, bf16[256,1024]{1,0:T(8,128)(2,1)S(1)}, u32[]{:S(2)}, u32[]{:S(2)}) collective-permute-start(bf16[256,1024]{1,0:T(8,128)(2,1)} %get-tuple-element.873), channel_id=1, source_target_pairs={{0,1},{1,2},{2,3},{3,4},{4,5},{5,6},{6,7},{7,8},{8,9},{9,10},{10,1... | collective-permute-start | bytes 1572872 | tf_op jit(solution)/shard_map/while/body/eval_jaxpr/ppermute | solution.py:22
  488.2 12.4 %collective-permute-start = (bf16[256,1024]{1,0:T(8,128)(2,1)}, bf16[256,1024]{1,0:T(8,128)(2,1)S(1)}, u32[]{:S(2)}, u32[]{:S(2)}) collective-permute-start(bf16[256,1024]{1,0:T(8,128)(2,1)} %get-tuple-element.873), channel_id=1, source_target_pairs={{0,1},{1,2},{2,3},{3,4},{4,5},{5,6},{6,7},{7,8},{8,9},{9,10},{10,1... | collective-permute-start | bytes 1572872 | tf_op jit(solution)/shard_map/while/body/eval_jaxpr/ppermute | solution.py:22
  502.7 1.4 copy-start.1
  506.6 12.4 %collective-permute-start = (bf16[256,1024]{1,0:T(8,128)(2,1)}, bf16[256,1024]{1,0:T(8,128)(2,1)S(1)}, u32[]{:S(2)}, u32[]{:S(2)}) collective-permute-start(bf16[256,1024]{1,0:T(8,128)(2,1)} %get-tuple-element.873), channel_id=1, source_target_pairs={{0,1},{1,2},{2,3},{3,4},{4,5},{5,6},{6,7},{7,8},{8,9},{9,10},{10,1... | collective-permute-start | bytes 1572872 | tf_op jit(solution)/shard_map/while/body/eval_jaxpr/ppermute | solution.py:22
  525.0 12.4 %collective-permute-start = (bf16[256,1024]{1,0:T(8,128)(2,1)}, bf16[256,1024]{1,0:T(8,128)(2,1)S(1)}, u32[]{:S(2)}, u32[]{:S(2)}) collective-permute-start(bf16[256,1024]{1,0:T(8,128)(2,1)} %get-tuple-element.873), channel_id=1, source_target_pairs={{0,1},{1,2},{2,3},{3,4},{4,5},{5,6},{6,7},{7,8},{8,9},{9,10},{10,1... | collective-permute-start | bytes 1572872 | tf_op jit(solution)/shard_map/while/body/eval_jaxpr/ppermute | solution.py:22
  543.5 12.4 %collective-permute-start = (bf16[256,1024]{1,0:T(8,128)(2,1)}, bf16[256,1024]{1,0:T(8,128)(2,1)S(1)}, u32[]{:S(2)}, u32[]{:S(2)}) collective-permute-start(bf16[256,1024]{1,0:T(8,128)(2,1)} %get-tuple-element.873), channel_id=1, source_target_pairs={{0,1},{1,2},{2,3},{3,4},{4,5},{5,6},{6,7},{7,8},{8,9},{9,10},{10,1... | collective-permute-start | bytes 1572872 | tf_op jit(solution)/shard_map/while/body/eval_jaxpr/ppermute | solution.py:22
  561.9 12.4 %collective-permute-start = (bf16[256,1024]{1,0:T(8,128)(2,1)}, bf16[256,1024]{1,0:T(8,128)(2,1)S(1)}, u32[]{:S(2)}, u32[]{:S(2)}) collective-permute-start(bf16[256,1024]{1,0:T(8,128)(2,1)} %get-tuple-element.873), channel_id=1, source_target_pairs={{0,1},{1,2},{2,3},{3,4},{4,5},{5,6},{6,7},{7,8},{8,9},{9,10},{10,1... | collective-permute-start | bytes 1572872 | tf_op jit(solution)/shard_map/while/body/eval_jaxpr/ppermute | solution.py:22
  580.3 12.4 %collective-permute-start = (bf16[256,1024]{1,0:T(8,128)(2,1)}, bf16[256,1024]{1,0:T(8,128)(2,1)S(1)}, u32[]{:S(2)}, u32[]{:S(2)}) collective-permute-start(bf16[256,1024]{1,0:T(8,128)(2,1)} %get-tuple-element.873), channel_id=1, source_target_pairs={{0,1},{1,2},{2,3},{3,4},{4,5},{5,6},{6,7},{7,8},{8,9},{9,10},{10,1... | collective-permute-start | bytes 1572872 | tf_op jit(solution)/shard_map/while/body/eval_jaxpr/ppermute | solution.py:22
  598.7 12.4 %collective-permute-start = (bf16[256,1024]{1,0:T(8,128)(2,1)}, bf16[256,1024]{1,0:T(8,128)(2,1)S(1)}, u32[]{:S(2)}, u32[]{:S(2)}) collective-permute-start(bf16[256,1024]{1,0:T(8,128)(2,1)} %get-tuple-element.873), channel_id=1, source_target_pairs={{0,1},{1,2},{2,3},{3,4},{4,5},{5,6},{6,7},{7,8},{8,9},{9,10},{10,1... | collective-permute-start | bytes 1572872 | tf_op jit(solution)/shard_map/while/body/eval_jaxpr/ppermute | solution.py:22
  613.3 1.4 copy-start.1
  617.2 12.4 %collective-permute-start = (bf16[256,1024]{1,0:T(8,128)(2,1)}, bf16[256,1024]{1,0:T(8,128)(2,1)S(1)}, u32[]{:S(2)}, u32[]{:S(2)}) collective-permute-start(bf16[256,1024]{1,0:T(8,128)(2,1)} %get-tuple-element.873), channel_id=1, source_target_pairs={{0,1},{1,2},{2,3},{3,4},{4,5},{5,6},{6,7},{7,8},{8,9},{9,10},{10,1... | collective-permute-start | bytes 1572872 | tf_op jit(solution)/shard_map/while/body/eval_jaxpr/ppermute | solution.py:22
  631.7 1.4 copy-start.1
  635.6 12.4 %collective-permute-start = (bf16[256,1024]{1,0:T(8,128)(2,1)}, bf16[256,1024]{1,0:T(8,128)(2,1)S(1)}, u32[]{:S(2)}, u32[]{:S(2)}) collective-permute-start(bf16[256,1024]{1,0:T(8,128)(2,1)} %get-tuple-element.873), channel_id=1, source_target_pairs={{0,1},{1,2},{2,3},{3,4},{4,5},{5,6},{6,7},{7,8},{8,9},{9,10},{10,1... | collective-permute-start | bytes 1572872 | tf_op jit(solution)/shard_map/while/body/eval_jaxpr/ppermute | solution.py:22
  654.0 12.4 %collective-permute-start = (bf16[256,1024]{1,0:T(8,128)(2,1)}, bf16[256,1024]{1,0:T(8,128)(2,1)S(1)}, u32[]{:S(2)}, u32[]{:S(2)}) collective-permute-start(bf16[256,1024]{1,0:T(8,128)(2,1)} %get-tuple-element.873), channel_id=1, source_target_pairs={{0,1},{1,2},{2,3},{3,4},{4,5},{5,6},{6,7},{7,8},{8,9},{9,10},{10,1... | collective-permute-start | bytes 1572872 | tf_op jit(solution)/shard_map/while/body/eval_jaxpr/ppermute | solution.py:22
  672.4 12.4 %collective-permute-start = (bf16[256,1024]{1,0:T(8,128)(2,1)}, bf16[256,1024]{1,0:T(8,128)(2,1)S(1)}, u32[]{:S(2)}, u32[]{:S(2)}) collective-permute-start(bf16[256,1024]{1,0:T(8,128)(2,1)} %get-tuple-element.873), channel_id=1, source_target_pairs={{0,1},{1,2},{2,3},{3,4},{4,5},{5,6},{6,7},{7,8},{8,9},{9,10},{10,1... | collective-permute-start | bytes 1572872 | tf_op jit(solution)/shard_map/while/body/eval_jaxpr/ppermute | solution.py:22
  690.9 12.4 %collective-permute-start = (bf16[256,1024]{1,0:T(8,128)(2,1)}, bf16[256,1024]{1,0:T(8,128)(2,1)S(1)}, u32[]{:S(2)}, u32[]{:S(2)}) collective-permute-start(bf16[256,1024]{1,0:T(8,128)(2,1)} %get-tuple-element.873), channel_id=1, source_target_pairs={{0,1},{1,2},{2,3},{3,4},{4,5},{5,6},{6,7},{7,8},{8,9},{9,10},{10,1... | collective-permute-start | bytes 1572872 | tf_op jit(solution)/shard_map/while/body/eval_jaxpr/ppermute | solution.py:22
  709.3 12.4 %collective-permute-start = (bf16[256,1024]{1,0:T(8,128)(2,1)}, bf16[256,1024]{1,0:T(8,128)(2,1)S(1)}, u32[]{:S(2)}, u32[]{:S(2)}) collective-permute-start(bf16[256,1024]{1,0:T(8,128)(2,1)} %get-tuple-element.873), channel_id=1, source_target_pairs={{0,1},{1,2},{2,3},{3,4},{4,5},{5,6},{6,7},{7,8},{8,9},{9,10},{10,1... | collective-permute-start | bytes 1572872 | tf_op jit(solution)/shard_map/while/body/eval_jaxpr/ppermute | solution.py:22
  727.7 12.4 %collective-permute-start = (bf16[256,1024]{1,0:T(8,128)(2,1)}, bf16[256,1024]{1,0:T(8,128)(2,1)S(1)}, u32[]{:S(2)}, u32[]{:S(2)}) collective-permute-start(bf16[256,1024]{1,0:T(8,128)(2,1)} %get-tuple-element.873), channel_id=1, source_target_pairs={{0,1},{1,2},{2,3},{3,4},{4,5},{5,6},{6,7},{7,8},{8,9},{9,10},{10,1... | collective-permute-start | bytes 1572872 | tf_op jit(solution)/shard_map/while/body/eval_jaxpr/ppermute | solution.py:22
  742.3 1.4 copy-start.1
  746.1 1.7 copy-start.6
  746.2 2.2 copy-start.3
  (86 other events, 88.6 us)
Sparse Core Ops, SparseCore 0:
  10.4 426.0 all-gather.1
where the time goes:
time: 759 us; the launch traced here: 757 us
  waiting for transfers between devices  568 us (75%)
  matrix products  69.1 us (9%)
  local copies, waits for them, and re-layouts  49.7 us (7%)
  other arithmetic  29.4 us (4%)
  between operations  14.9 us (2%)
  blocking collectives  14.1 us (2%)
  loops' own time  12.3 us (2%)
    all_gather x1, waiting for transfers between devices, local(): lax.all_gather(fresh_weight, ('dp', 'ctx'), axis=0, tiled=True)  402 us
    ppermute x15, waiting for transfers between devices, passed_along(): return lax.ppermute(x, axis, [(i, (i + by) % count) for i in range(count)])  166 us
    dot_general x64, matrix products, attend_head(): jnp.einsum('jqk,kd->jqd', weights.astype(jnp.bfloat16), value_part, prefe...  38.3 us
    while x255, local copies, waits for them, and re-layouts  24.8 us
    dot_general x64, matrix products, attend_head(): jnp.einsum('qjd,kd->jqk', group_q, key_part, preferred_element_type=jnp.f...  21.1 us
  transfers between devices with their start and end apart: 16, of which 16 were waited for; matrix products, arithmetic and copies ran while one was open for 3% of the time, Pallas kernels for 0%

commit v1 on v0

--- a/solution.py
+++ b/solution.py
@@ -58,7 +58,12 @@
     block_len = tok_rows.shape[0]
     projected = jnp.dot(
         tok_rows,
-        lax.all_gather(fresh_weight, ("dp", "ctx"), axis=0, tiled=True),
+        jnp.concatenate(
+            lax.all_to_all(
+                jnp.stack([fresh_weight] * lax.axis_size(("dp", "ctx"))), ("dp", "ctx"), 0, 0
+            ),
+            axis=0,
+        ),
         preferred_element_type=jnp.float32,
     )
     place = lax.axis_index("ctx")

time: 759 us -> 617 us (0.81)
  waiting for transfers between devices: 568 us -> 400 us
  blocking collectives: 14.1 us -> 35.9 us
  starting transfers between devices: 0.08 us -> 15.3 us
  between operations: 14.9 us -> 1.57 us
    all_gather x1 -> x0, waiting for transfers between devices: 402 us -> none  [local(): lax.all_gather(fresh_weight, ('dp', 'ctx'), axis=0, tiled=True)]
    all_to_all x0 -> x1, waiting for transfers between devices: none -> 234 us  [local(): lax.all_to_all(jnp.stack([fresh_weight] * lax.axis_size(('dp', 'ctx'))),...]
    unnamed x1, blocking collectives: 14.1 us -> 35.9 us
    all_to_all x0 -> x1, starting transfers between devices: none -> 15.3 us  [local(): lax.all_to_all(jnp.stack([fresh_weight] * lax.axis_size(('dp', 'ctx'))),...]
where the time goes in v1:
time: 617 us; the launch traced here: 616 us
  waiting for transfers between devices  400 us (65%)
  matrix products  69.1 us (11%)
  local copies, waits for them, and re-layouts  54.5 us (9%)
  blocking collectives  35.9 us (6%)
  other arithmetic  27.5 us (4%)
  starting transfers between devices  15.3 us (2%)
  loops' own time  12.3 us (2%)
    all_to_all x1, waiting for transfers between devices, local(): lax.all_to_all(jnp.stack([fresh_weight] * lax.axis_size(('dp', 'ctx'))),...  234 us
    ppermute x15, waiting for transfers between devices, passed_along(): return lax.ppermute(x, axis, [(i, (i + by) % count) for i in range(count)])  166 us
    dot_general x64, matrix products, attend_head(): jnp.einsum('jqk,kd->jqd', weights.astype(jnp.bfloat16), value_part, prefe...  38.3 us
    unnamed x1, blocking collectives  35.9 us
    while x255, local copies, waits for them, and re-layouts  24.8 us
    dot_general x64, matrix products, attend_head(): jnp.einsum('qjd,kd->jqk', group_q, key_part, preferred_element_type=jnp.f...  21.1 us
    all_to_all x1, starting transfers between devices, local(): lax.all_to_all(jnp.stack([fresh_weight] * lax.axis_size(('dp', 'ctx'))),...  15.3 us
  transfers between devices with their start and end apart: 16, of which 16 were waited for; matrix products, arithmetic and copies ran while one was open for 3% of the time, Pallas kernels for 0%

profile of v1, /device:TPU:32, one launch (start us, length us, event | category | flops | bytes accessed | tf_op | source)
XLA Modules:
  0.0 615.9 jit_solution(7038033841974025035)
XLA Ops:
  2.5 6.1 stack.2
  8.6 15.3 %all-to-all-start = ((bf16[256,8,3072]{2,1,0:T(8,128)(2,1)}), bf16[256,8,3072]{2,1,0:T(8,128)(2,1)}, u32[]{:S(2)}, u32[]{:S(2)}) async-start(bf16[256,8,3072]{2,1,0:T(8,128)(2,1)} %stack.2), calls=%async_computation | async-start | bytes 25165824 | tf_op jit(solution)/shard_map/all_to_all | solution.py:62
  29.6 35.9 %all-reduce = s32[16]{0:T(128)S(1)} all-reduce(s32[16]{0:T(128)S(1)} %dynamic-update-slice), channel_id=1, replica_groups=mesh['dp'=16,'ctx'=16] {'ctx'}, use_global_device_ids=true, to_apply=%add | all-reduce | flops 16 | bytes 128
  67.9 234.0 %all-to-all-done = bf16[256,8,3072]{2,1,0:T(8,128)(2,1)} async-done(((bf16[256,8,3072]{2,1,0:T(8,128)(2,1)}), bf16[256,8,3072]{2,1,0:T(8,128)(2,1)}, u32[]{:S(2)}, u32[]{:S(2)}) %all-to-all-start) | async-done | bytes 12582944 | tf_op jit(solution)/shard_map/all_to_all | solution.py:62
  301.9 9.7 %fusion.123 = (bf16[256,3072]{0,1:T(8,128)(2,1)}, f32[256,3072]{0,1:T(8,128)S(1)}) fusion(bf16[1,256,2048]{2,1,0:T(8,128)(2,1)S(1)} %copy-done, bf16[256,8,3072]{2,1,0:T(8,128)(2,1)} %all-to-all-done), kind=kOutput, calls=%fused_computation.204 | convolution fusion | flops 3222011904 | bytes 18350080 | tf_op jit(solution)/shard_map/dot_general | solution.py:59
  315.9 3.2 copy.111
  320.2 2.2 add_convert_fusion
  332.0 2.1 convolution_add_fusion.4
  335.1 276.4 %while.40 = (s32[]{:T(128)}, f32[4,256]{1,0:T(4,128)S(1)}, f32[4,256]{1,0:T(4,128)S(1)}, f32[4,256,128]{2,1,0:T(8,128)S(1)}, f32[4,256]{1,0:T(4,128)S(1)}, /*ind...) while((s32[]{:T(128)}, f32[4,256]{1,0:T(4,128)S(1)}, ...), condition=%wide.region_21.22_spmd.clone, body=%wide.region_12.21_spmd.clone.sunk | while | flops 547561984 | bytes 35001972 | solution.py:138
  336.5 11.1 %collective-permute-done = bf16[256,1024]{1,0:T(8,128)(2,1)S(1)} collective-permute-done((bf16[256,1024]{1,0:T(8,128)(2,1)}, bf16[256,1024]{1,0:T(8,128)(2,1)S(1)}, u32[]{:S(2)}, u32[]{:S(2)}) %collective-permute-start) | collective-permute-done | bytes 524320 | tf_op jit(solution)/shard_map/while/body/eval_jaxpr/ppermute | solution.py:22
  354.9 11.1 %collective-permute-done = bf16[256,1024]{1,0:T(8,128)(2,1)S(1)} collective-permute-done((bf16[256,1024]{1,0:T(8,128)(2,1)}, bf16[256,1024]{1,0:T(8,128)(2,1)S(1)}, u32[]{:S(2)}, u32[]{:S(2)}) %collective-permute-start) | collective-permute-done | bytes 524320 | tf_op jit(solution)/shard_map/while/body/eval_jaxpr/ppermute | solution.py:22
  373.4 11.1 %collective-permute-done = bf16[256,1024]{1,0:T(8,128)(2,1)S(1)} collective-permute-done((bf16[256,1024]{1,0:T(8,128)(2,1)}, bf16[256,1024]{1,0:T(8,128)(2,1)S(1)}, u32[]{:S(2)}, u32[]{:S(2)}) %collective-permute-start) | collective-permute-done | bytes 524320 | tf_op jit(solution)/shard_map/while/body/eval_jaxpr/ppermute | solution.py:22
  391.8 11.1 %collective-permute-done = bf16[256,1024]{1,0:T(8,128)(2,1)S(1)} collective-permute-done((bf16[256,1024]{1,0:T(8,128)(2,1)}, bf16[256,1024]{1,0:T(8,128)(2,1)S(1)}, u32[]{:S(2)}, u32[]{:S(2)}) %collective-permute-start) | collective-permute-done | bytes 524320 | tf_op jit(solution)/shard_map/while/body/eval_jaxpr/ppermute | solution.py:22
  410.2 11.1 %collective-permute-done = bf16[256,1024]{1,0:T(8,128)(2,1)S(1)} collective-permute-done((bf16[256,1024]{1,0:T(8,128)(2,1)}, bf16[256,1024]{1,0:T(8,128)(2,1)S(1)}, u32[]{:S(2)}, u32[]{:S(2)}) %collective-permute-start) | collective-permute-done | bytes 524320 | tf_op jit(solution)/shard_map/while/body/eval_jaxpr/ppermute | solution.py:22
  428.6 11.1 %collective-permute-done = bf16[256,1024]{1,0:T(8,128)(2,1)S(1)} collective-permute-done((bf16[256,1024]{1,0:T(8,128)(2,1)}, bf16[256,1024]{1,0:T(8,128)(2,1)S(1)}, u32[]{:S(2)}, u32[]{:S(2)}) %collective-permute-start) | collective-permute-done | bytes 524320 | tf_op jit(solution)/shard_map/while/body/eval_jaxpr/ppermute | solution.py:22
  447.1 11.1 %collective-permute-done = bf16[256,1024]{1,0:T(8,128)(2,1)S(1)} collective-permute-done((bf16[256,1024]{1,0:T(8,128)(2,1)}, bf16[256,1024]{1,0:T(8,128)(2,1)S(1)}, u32[]{:S(2)}, u32[]{:S(2)}) %collective-permute-start) | collective-permute-done | bytes 524320 | tf_op jit(solution)/shard_map/while/body/eval_jaxpr/ppermute | solution.py:22
  465.5 11.1 %collective-permute-done = bf16[256,1024]{1,0:T(8,128)(2,1)S(1)} collective-permute-done((bf16[256,1024]{1,0:T(8,128)(2,1)}, bf16[256,1024]{1,0:T(8,128)(2,1)S(1)}, u32[]{:S(2)}, u32[]{:S(2)}) %collective-permute-start) | collective-permute-done | bytes 524320 | tf_op jit(solution)/shard_map/while/body/eval_jaxpr/ppermute | solution.py:22
  483.9 11.1 %collective-permute-done = bf16[256,1024]{1,0:T(8,128)(2,1)S(1)} collective-permute-done((bf16[256,1024]{1,0:T(8,128)(2,1)}, bf16[256,1024]{1,0:T(8,128)(2,1)S(1)}, u32[]{:S(2)}, u32[]{:S(2)}) %collective-permute-start) | collective-permute-done | bytes 524320 | tf_op jit(solution)/shard_map/while/body/eval_jaxpr/ppermute | solution.py:22
  502.3 11.1 %collective-permute-done = bf16[256,1024]{1,0:T(8,128)(2,1)S(1)} collective-permute-done((bf16[256,1024]{1,0:T(8,128)(2,1)}, bf16[256,1024]{1,0:T(8,128)(2,1)S(1)}, u32[]{:S(2)}, u32[]{:S(2)}) %collective-permute-start) | collective-permute-done | bytes 524320 | tf_op jit(solution)/shard_map/while/body/eval_jaxpr/ppermute | solution.py:22
  520.8 11.1 %collective-permute-done = bf16[256,1024]{1,0:T(8,128)(2,1)S(1)} collective-permute-done((bf16[256,1024]{1,0:T(8,128)(2,1)}, bf16[256,1024]{1,0:T(8,128)(2,1)S(1)}, u32[]{:S(2)}, u32[]{:S(2)}) %collective-permute-start) | collective-permute-done | bytes 524320 | tf_op jit(solution)/shard_map/while/body/eval_jaxpr/ppermute | solution.py:22
  539.2 11.1 %collective-permute-done = bf16[256,1024]{1,0:T(8,128)(2,1)S(1)} collective-permute-done((bf16[256,1024]{1,0:T(8,128)(2,1)}, bf16[256,1024]{1,0:T(8,128)(2,1)S(1)}, u32[]{:S(2)}, u32[]{:S(2)}) %collective-permute-start) | collective-permute-done | bytes 524320 | tf_op jit(solution)/shard_map/while/body/eval_jaxpr/ppermute | solution.py:22
  557.6 11.1 %collective-permute-done = bf16[256,1024]{1,0:T(8,128)(2,1)S(1)} collective-permute-done((bf16[256,1024]{1,0:T(8,128)(2,1)}, bf16[256,1024]{1,0:T(8,128)(2,1)S(1)}, u32[]{:S(2)}, u32[]{:S(2)}) %collective-permute-start) | collective-permute-done | bytes 524320 | tf_op jit(solution)/shard_map/while/body/eval_jaxpr/ppermute | solution.py:22
  576.0 11.1 %collective-permute-done = bf16[256,1024]{1,0:T(8,128)(2,1)S(1)} collective-permute-done((bf16[256,1024]{1,0:T(8,128)(2,1)}, bf16[256,1024]{1,0:T(8,128)(2,1)S(1)}, u32[]{:S(2)}, u32[]{:S(2)}) %collective-permute-start) | collective-permute-done | bytes 524320 | tf_op jit(solution)/shard_map/while/body/eval_jaxpr/ppermute | solution.py:22
  594.5 11.1 %collective-permute-done = bf16[256,1024]{1,0:T(8,128)(2,1)S(1)} collective-permute-done((bf16[256,1024]{1,0:T(8,128)(2,1)}, bf16[256,1024]{1,0:T(8,128)(2,1)S(1)}, u32[]{:S(2)}, u32[]{:S(2)}) %collective-permute-start) | collective-permute-done | bytes 524320 | tf_op jit(solution)/shard_map/while/body/eval_jaxpr/ppermute | solution.py:22
  (625 shorter events, 127.9 us)
Async XLA Ops:
  0.6 301.2 %copy-start = (bf16[1,256,2048]{2,1,0:T(8,128)(2,1)S(1)}, bf16[1,256,2048]{2,1,0:T(8,128)(2,1)}, u32[]{:S(2)}) copy-start(bf16[1,256,2048]{2,1,0:T(8,128)(2,1)} %param.9) | copy-start | bytes 3145732
  8.6 15.3 %copy-start.10 = (s32[16]{0:T(128)S(1)}, s32[16]{0:T(128)}, u32[]{:S(2)}) copy-start(s32[16]{0:T(128)} %param.11) | copy-start | bytes 196
  8.6 16.5 %copy-start.9 = (s32[1,256]{1,0:T(1,128)S(1)}, s32[1,256]{1,0:T(1,128)}, u32[]{:S(2)}) copy-start(s32[1,256]{1,0:T(1,128)} %param.10) | copy-start | bytes 3076
  8.6 18.9 %copy-start.11 = (u32[256]{0:T(256)S(1)}, u32[256]{0:T(256)}, u32[]{:S(2)}) copy-start(u32[256]{0:T(256)} %constant.170) | copy-start | bytes 3076
  8.6 293.3 %all-to-all-start = ((bf16[256,8,3072]{2,1,0:T(8,128)(2,1)}), bf16[256,8,3072]{2,1,0:T(8,128)(2,1)}, u32[]{:S(2)}, u32[]{:S(2)}) async-start(bf16[256,8,3072]{2,1,0:T(8,128)(2,1)} %stack.2), calls=%async_computation | async-start | bytes 25165824 | tf_op jit(solution)/shard_map/all_to_all | solution.py:62
  335.1 12.4 %collective-permute-start = (bf16[256,1024]{1,0:T(8,128)(2,1)}, bf16[256,1024]{1,0:T(8,128)(2,1)S(1)}, u32[]{:S(2)}, u32[]{:S(2)}) collective-permute-start(bf16[256,1024]{1,0:T(8,128)(2,1)} %get-tuple-element.873), channel_id=1, source_target_pairs={{0,1},{1,2},{2,3},{3,4},{4,5},{5,6},{6,7},{7,8},{8,9},{9,10},{10,1... | collective-permute-start | bytes 1572872 | tf_op jit(solution)/shard_map/while/body/eval_jaxpr/ppermute | solution.py:22
  353.6 12.4 %collective-permute-start = (bf16[256,1024]{1,0:T(8,128)(2,1)}, bf16[256,1024]{1,0:T(8,128)(2,1)S(1)}, u32[]{:S(2)}, u32[]{:S(2)}) collective-permute-start(bf16[256,1024]{1,0:T(8,128)(2,1)} %get-tuple-element.873), channel_id=1, source_target_pairs={{0,1},{1,2},{2,3},{3,4},{4,5},{5,6},{6,7},{7,8},{8,9},{9,10},{10,1... | collective-permute-start | bytes 1572872 | tf_op jit(solution)/shard_map/while/body/eval_jaxpr/ppermute | solution.py:22
  372.0 12.4 %collective-permute-start = (bf16[256,1024]{1,0:T(8,128)(2,1)}, bf16[256,1024]{1,0:T(8,128)(2,1)S(1)}, u32[]{:S(2)}, u32[]{:S(2)}) collective-permute-start(bf16[256,1024]{1,0:T(8,128)(2,1)} %get-tuple-element.873), channel_id=1, source_target_pairs={{0,1},{1,2},{2,3},{3,4},{4,5},{5,6},{6,7},{7,8},{8,9},{9,10},{10,1... | collective-permute-start | bytes 1572872 | tf_op jit(solution)/shard_map/while/body/eval_jaxpr/ppermute | solution.py:22
  390.4 12.4 %collective-permute-start = (bf16[256,1024]{1,0:T(8,128)(2,1)}, bf16[256,1024]{1,0:T(8,128)(2,1)S(1)}, u32[]{:S(2)}, u32[]{:S(2)}) collective-permute-start(bf16[256,1024]{1,0:T(8,128)(2,1)} %get-tuple-element.873), channel_id=1, source_target_pairs={{0,1},{1,2},{2,3},{3,4},{4,5},{5,6},{6,7},{7,8},{8,9},{9,10},{10,1... | collective-permute-start | bytes 1572872 | tf_op jit(solution)/shard_map/while/body/eval_jaxpr/ppermute | solution.py:22
  408.8 12.4 %collective-permute-start = (bf16[256,1024]{1,0:T(8,128)(2,1)}, bf16[256,1024]{1,0:T(8,128)(2,1)S(1)}, u32[]{:S(2)}, u32[]{:S(2)}) collective-permute-start(bf16[256,1024]{1,0:T(8,128)(2,1)} %get-tuple-element.873), channel_id=1, source_target_pairs={{0,1},{1,2},{2,3},{3,4},{4,5},{5,6},{6,7},{7,8},{8,9},{9,10},{10,1... | collective-permute-start | bytes 1572872 | tf_op jit(solution)/shard_map/while/body/eval_jaxpr/ppermute | solution.py:22
  423.4 1.4 copy-start.1
  427.3 12.4 %collective-permute-start = (bf16[256,1024]{1,0:T(8,128)(2,1)}, bf16[256,1024]{1,0:T(8,128)(2,1)S(1)}, u32[]{:S(2)}, u32[]{:S(2)}) collective-permute-start(bf16[256,1024]{1,0:T(8,128)(2,1)} %get-tuple-element.873), channel_id=1, source_target_pairs={{0,1},{1,2},{2,3},{3,4},{4,5},{5,6},{6,7},{7,8},{8,9},{9,10},{10,1... | collective-permute-start | bytes 1572872 | tf_op jit(solution)/shard_map/while/body/eval_jaxpr/ppermute | solution.py:22
  445.7 12.4 %collective-permute-start = (bf16[256,1024]{1,0:T(8,128)(2,1)}, bf16[256,1024]{1,0:T(8,128)(2,1)S(1)}, u32[]{:S(2)}, u32[]{:S(2)}) collective-permute-start(bf16[256,1024]{1,0:T(8,128)(2,1)} %get-tuple-element.873), channel_id=1, source_target_pairs={{0,1},{1,2},{2,3},{3,4},{4,5},{5,6},{6,7},{7,8},{8,9},{9,10},{10,1... | collective-permute-start | bytes 1572872 | tf_op jit(solution)/shard_map/while/body/eval_jaxpr/ppermute | solution.py:22
  464.1 12.4 %collective-permute-start = (bf16[256,1024]{1,0:T(8,128)(2,1)}, bf16[256,1024]{1,0:T(8,128)(2,1)S(1)}, u32[]{:S(2)}, u32[]{:S(2)}) collective-permute-start(bf16[256,1024]{1,0:T(8,128)(2,1)} %get-tuple-element.873), channel_id=1, source_target_pairs={{0,1},{1,2},{2,3},{3,4},{4,5},{5,6},{6,7},{7,8},{8,9},{9,10},{10,1... | collective-permute-start | bytes 1572872 | tf_op jit(solution)/shard_map/while/body/eval_jaxpr/ppermute | solution.py:22
  482.5 12.4 %collective-permute-start = (bf16[256,1024]{1,0:T(8,128)(2,1)}, bf16[256,1024]{1,0:T(8,128)(2,1)S(1)}, u32[]{:S(2)}, u32[]{:S(2)}) collective-permute-start(bf16[256,1024]{1,0:T(8,128)(2,1)} %get-tuple-element.873), channel_id=1, source_target_pairs={{0,1},{1,2},{2,3},{3,4},{4,5},{5,6},{6,7},{7,8},{8,9},{9,10},{10,1... | collective-permute-start | bytes 1572872 | tf_op jit(solution)/shard_map/while/body/eval_jaxpr/ppermute | solution.py:22
  501.0 12.4 %collective-permute-start = (bf16[256,1024]{1,0:T(8,128)(2,1)}, bf16[256,1024]{1,0:T(8,128)(2,1)S(1)}, u32[]{:S(2)}, u32[]{:S(2)}) collective-permute-start(bf16[256,1024]{1,0:T(8,128)(2,1)} %get-tuple-element.873), channel_id=1, source_target_pairs={{0,1},{1,2},{2,3},{3,4},{4,5},{5,6},{6,7},{7,8},{8,9},{9,10},{10,1... | collective-permute-start | bytes 1572872 | tf_op jit(solution)/shard_map/while/body/eval_jaxpr/ppermute | solution.py:22
  519.4 12.4 %collective-permute-start = (bf16[256,1024]{1,0:T(8,128)(2,1)}, bf16[256,1024]{1,0:T(8,128)(2,1)S(1)}, u32[]{:S(2)}, u32[]{:S(2)}) collective-permute-start(bf16[256,1024]{1,0:T(8,128)(2,1)} %get-tuple-element.873), channel_id=1, source_target_pairs={{0,1},{1,2},{2,3},{3,4},{4,5},{5,6},{6,7},{7,8},{8,9},{9,10},{10,1... | collective-permute-start | bytes 1572872 | tf_op jit(solution)/shard_map/while/body/eval_jaxpr/ppermute | solution.py:22
  533.9 1.4 copy-start.1
  537.8 12.4 %collective-permute-start = (bf16[256,1024]{1,0:T(8,128)(2,1)}, bf16[256,1024]{1,0:T(8,128)(2,1)S(1)}, u32[]{:S(2)}, u32[]{:S(2)}) collective-permute-start(bf16[256,1024]{1,0:T(8,128)(2,1)} %get-tuple-element.873), channel_id=1, source_target_pairs={{0,1},{1,2},{2,3},{3,4},{4,5},{5,6},{6,7},{7,8},{8,9},{9,10},{10,1... | collective-permute-start | bytes 1572872 | tf_op jit(solution)/shard_map/while/body/eval_jaxpr/ppermute | solution.py:22
  556.2 12.4 %collective-permute-start = (bf16[256,1024]{1,0:T(8,128)(2,1)}, bf16[256,1024]{1,0:T(8,128)(2,1)S(1)}, u32[]{:S(2)}, u32[]{:S(2)}) collective-permute-start(bf16[256,1024]{1,0:T(8,128)(2,1)} %get-tuple-element.873), channel_id=1, source_target_pairs={{0,1},{1,2},{2,3},{3,4},{4,5},{5,6},{6,7},{7,8},{8,9},{9,10},{10,1... | collective-permute-start | bytes 1572872 | tf_op jit(solution)/shard_map/while/body/eval_jaxpr/ppermute | solution.py:22
  574.7 12.4 %collective-permute-start = (bf16[256,1024]{1,0:T(8,128)(2,1)}, bf16[256,1024]{1,0:T(8,128)(2,1)S(1)}, u32[]{:S(2)}, u32[]{:S(2)}) collective-permute-start(bf16[256,1024]{1,0:T(8,128)(2,1)} %get-tuple-element.873), channel_id=1, source_target_pairs={{0,1},{1,2},{2,3},{3,4},{4,5},{5,6},{6,7},{7,8},{8,9},{9,10},{10,1... | collective-permute-start | bytes 1572872 | tf_op jit(solution)/shard_map/while/body/eval_jaxpr/ppermute | solution.py:22
  593.1 12.4 %collective-permute-start = (bf16[256,1024]{1,0:T(8,128)(2,1)}, bf16[256,1024]{1,0:T(8,128)(2,1)S(1)}, u32[]{:S(2)}, u32[]{:S(2)}) collective-permute-start(bf16[256,1024]{1,0:T(8,128)(2,1)} %get-tuple-element.873), channel_id=1, source_target_pairs={{0,1},{1,2},{2,3},{3,4},{4,5},{5,6},{6,7},{7,8},{8,9},{9,10},{10,1... | collective-permute-start | bytes 1572872 | tf_op jit(solution)/shard_map/while/body/eval_jaxpr/ppermute | solution.py:22
  611.5 1.7 copy-start.6
  611.5 2.2 copy-start.3
  (88 other events, 91.5 us)
